TPU v7x, 128 devices: a whole 4x4x4 slice. The times are simulated.
128 devices in a mesh: tm: 4 (over z_hi, core), pair: 32 (over z_lo, y, x).
Axes of the slice: x: 4, y: 4, z: 4 (z_hi: 2, z_lo: 2; z = z_hi * 2 + z_lo), core: 2. Of those that a mesh axis runs over, the one named last changes fastest.
Arguments:
- orbitals: bfloat16 [32768, 512], P('pair', 'tm'), may hold values from -1.5 to 1.5
- level_gap: float32 [512], replicated, may hold values from 0.05 to 1.5
- screened: bfloat16 [8, 128, 1024, 1024], P('tm', 'pair'), may hold values from -0.008972168 to 0.008972168
- pair_blocks: int32 [128, 2], P('pair'), may hold values from 0 to 31, as said below
Outputs:
- self_energy: float32 [8, 512, 512], P('tm', 'pair')
Inputs may be any that keep to these rules, and one draw needn't show every extreme that they name: `pair_blocks`: each row names two point blocks a <= c; no unordered pair appears in two rows; the pair (0, 31) appears in every draw.
All inputs are finite; a program needn't handle non-finite values.
Results may differ from a plain program's by a relative error of at most 0.0049.
Values may be sent and summed in bfloat16 or wider, within the bound.
No kernel may reach another device: no remote copies, remote signals or barrier semaphores. Data moves between devices by JAX's collectives and lax.ppermute only.
A program may use at most 128 MiB of HBM per device.

v0:
```python
import jax
import jax.numpy as jnp
from jax import lax
from jax.sharding import Mesh
from jax.sharding import PartitionSpec as P

NOCC = 128
PAIR = ("pair_0", "pair_1", "pair_2")


def laid_out(tiles, dim):
    tiles = jnp.moveaxis(tiles, 0, dim)
    shape = tiles.shape
    return tiles.reshape(*shape[:dim], shape[dim] * shape[dim + 1], *shape[dim + 2 :])


def stacked_from(array, axes, sequence):
    tiles = array[None]
    for k in sequence:
        tiles = lax.all_gather(tiles, axes[k], axis=0, tiled=True)
    carried = [lax.axis_size(axes[k]) for k in reversed(sequence)]
    tiles = tiles.reshape(*carried, *array.shape)
    turned = sorted(range(len(sequence)), key=lambda place: sequence[len(sequence) - 1 - place])
    return tiles.transpose(*turned, *range(len(sequence), tiles.ndim)).reshape(-1, *array.shape)


def whole_of(array, axes, sequence, dim):
    return laid_out(stacked_from(array, axes, sequence), dim)


def split_up(array, dim, count):
    shape = array.shape
    tiles = array.reshape(*shape[:dim], count, shape[dim] // count, *shape[dim + 1 :])
    return jnp.moveaxis(tiles, dim, 0)


def sum_at_owner(array, axis, dim):
    count = lax.axis_size(axis)
    tiles = lax.all_to_all(split_up(array, dim, count), axis, 0, 0, tiled=True)
    return jnp.sum(tiles, axis=0)


def shards(orbitals, level_gap, screened, pair_blocks):
    block_rows = orbitals.shape[0]
    wanted = pair_blocks.reshape(-1)
    narrow = whole_of(orbitals, PAIR, (0, 1, 2), 0)
    picked = jnp.take(narrow.reshape(-1, block_rows, narrow.shape[1]), wanted, axis=0)
    chosen = lax.all_gather(picked, "tm", axis=2, tiled=True)
    orbital_count = chosen.shape[2]
    time_local = screened.shape[0]
    pair_local = screened.shape[1]
    time_total = time_local * lax.axis_size("tm")
    first_time = lax.axis_index("tm") * time_local
    moments = (first_time + jnp.arange(time_local)).astype(jnp.float32)
    tau = 6.0 * (moments + 0.5) / time_total
    signs = jnp.where(jnp.arange(orbital_count) < NOCC, 1.0, -1.0).astype(jnp.float32)
    factors = signs[None, :] * jnp.exp(-level_gap[None, :] * tau[:, None])
    totals = []
    for time_step in range(time_local):
        total = jnp.zeros((orbital_count, orbital_count), jnp.float32)
        for pair_step in range(pair_local):
            left = chosen[2 * pair_step]
            right = chosen[2 * pair_step + 1]
            scaled = (left.astype(jnp.float32) * factors[time_step][None, :]).astype(jnp.bfloat16)
            green = lax.dot_general(
                scaled, right, (((1,), (1,)), ((), ())), preferred_element_type=jnp.float32
            )
            product = (green * screened[time_step, pair_step].astype(jnp.float32)).astype(
                jnp.bfloat16
            )
            half = lax.dot_general(
                left, product, (((0,), (0,)), ((), ())), preferred_element_type=jnp.float32
            ).astype(jnp.bfloat16)
            block = jnp.dot(half, right, preferred_element_type=jnp.float32)
            weight = jnp.where(
                pair_blocks[pair_step, 0] == pair_blocks[pair_step, 1], 0.5, 1.0
            ).astype(jnp.float32)
            total = total + weight * (block + block.T)
        totals.append(total)
    partial_sum = jnp.stack(totals, axis=0)
    return sum_at_owner(partial_sum, PAIR, 1)


def solution(mesh):
    finer = Mesh(
        mesh.devices.reshape(mesh.shape["tm"], 2, 4, 4), ("tm", "pair_0", "pair_1", "pair_2")
    )
    placed = (P(PAIR, "tm"), P(), P("tm", PAIR, None, None), P(PAIR, None))
    return jax.shard_map(
        shards, mesh=finer, in_specs=placed, out_specs=P("tm", PAIR, None), check_vma=False
    )
```

profile of v0, /device:TPU:0, one launch (start us, length us, event | category | flops | bytes accessed | tf_op | source)
XLA Modules:
  0.0 349.6 jit_solution(2108790576608835699)
XLA Ops:
  6.5 10.9 %all-gather = bf16[2048,128]{1,0:T(8,128)(2,1)} all-gather(bf16[1024,128]{1,0:T(8,128)(2,1)} %param.4), channel_id=2, replica_groups=mesh['tm'=4,'pair_0'=2,'pair_1'=4,'pair_2'=4] {'pair_0'}, dimensions={0}, use_global_device_ids=true | all-gather | bytes 786432 | tf_op jit(solution)/shard_map/all_gather | solution.py:20
  17.6 32.8 %all-gather.5.cloned.1.call-done = bf16[8,1024,128]{2,1,0:T(8,128)(2,1)} async-done(((bf16[2,1024,128]{2,1,0:T(8,128)(2,1)}), bf16[8,1024,128]{2,1,0:T(8,128)(2,1)}) %all-gather.5.cloned.1.call-update) | async-done | bytes 2097168 | tf_op jit(solution)/shard_map/all_gather | solution.py:20
  51.4 83.7 %all-gather.7.cloned.1.call-done = bf16[32,1024,128]{2,1,0:T(8,128)(2,1)} async-done(((bf16[8,1024,128]{2,1,0:T(8,128)(2,1)}), bf16[32,1024,128]{2,1,0:T(8,128)(2,1)}) %all-gather.7.cloned.1.call-update) | async-done | bytes 8388624 | tf_op jit(solution)/shard_map/all_gather | solution.py:20
  135.1 7.5 %copy.37 = bf16[2,4,4,1024,128]{4,3,2,1,0:T(8,128)(2,1)} copy(bf16[2,4,4,1024,128]{4,3,0,1,2:T(8,128)(2,1)} %bitcast.218) | data formatting | bytes 16777216 | tf_op jit(solution)/shard_map/transpose | solution.py:24
  142.6 4.3 %gather_fusion = bf16[8,1024,128]{2,1,0:T(8,128)(2,1)S(1)} fusion(bf16[32,1024,128]{2,1,0:T(8,128)(2,1)} %bitcast.217, s32[1024]{0:T(1024)S(1)} %pad_clamp_fusion), kind=kCustom, calls=%fused_computation | custom fusion | bytes 4194336 | tf_op jit(solution)/shard_map/jit(_take)/gather | solution.py:47
  154.5 58.9 %all-gather.9.cloned.1.call-done = bf16[8,1024,512]{2,1,0:T(8,128)(2,1)} async-done(((bf16[8,1024,128]{2,1,0:T(8,128)(2,1)}), bf16[8,1024,512]{2,1,0:T(8,128)(2,1)}) %all-gather.9.cloned.1.call-update) | async-done | bytes 8388624 | tf_op jit(solution)/shard_map/all_gather | solution.py:48
  213.4 4.9 %convolution_convert_fusion.3 = bf16[512,1024]{1,0:T(8,128)(2,1)S(1)} fusion(bf16[2,4,1024,1024]{3,2,1,0:T(8,128)(2,1)} %param.6, f32[512]{0:T(512)S(1)} %bitcast.226, bf16[8,1024,512]{2,1,0:T(8,128)(2,1)} %all-gather.9.cloned.1.call-done), kind=kOutput, calls=%fused_computation.38 | convolution fusion | flops 2152726528 | bytes 6293504 | tf_op jit(solution)/shard_map/dot_general | solution.py:71
  220.6 6.0 %convolution_convert_fusion.2 = bf16[512,1024]{1,0:T(8,128)(2,1)} fusion(bf16[2,4,1024,1024]{3,2,1,0:T(8,128)(2,1)} %param.6, f32[512]{0:T(512)S(1)} %bitcast.227, bf16[8,1024,512]{2,1,0:T(8,128)(2,1)} %all-gather.9.cloned.1.call-done), kind=kOutput, calls=%fused_computation.37 | convolution fusion | flops 2152726528 | bytes 6293504 | tf_op jit(solution)/shard_map/dot_general | solution.py:71
  230.2 5.9 %convolution_convert_fusion = bf16[512,1024]{1,0:T(8,128)(2,1)} fusion(bf16[2,4,1024,1024]{3,2,1,0:T(8,128)(2,1)} %param.6, f32[512]{0:T(512)S(1)} %bitcast.228, bf16[8,1024,512]{2,1,0:T(8,128)(2,1)} %all-gather.9.cloned.1.call-done), kind=kOutput, calls=%fused_computation.35 | convolution fusion | flops 2152726528 | bytes 6293504 | tf_op jit(solution)/shard_map/dot_general | solution.py:71
  236.1 3.2 fusion.108
  241.8 6.0 %convolution_convert_fusion.1 = bf16[512,1024]{1,0:T(8,128)(2,1)} fusion(bf16[2,4,1024,1024]{3,2,1,0:T(8,128)(2,1)} %param.6, f32[512]{0:T(512)S(1)} %bitcast.229, bf16[8,1024,512]{2,1,0:T(8,128)(2,1)} %all-gather.9.cloned.1.call-done), kind=kOutput, calls=%fused_computation.36 | convolution fusion | flops 2152726528 | bytes 6293504 | tf_op jit(solution)/shard_map/dot_general | solution.py:71
  247.8 3.2 fusion.106
  251.0 2.8 copy.45
  253.8 5.9 %convolution_convert_fusion.4 = bf16[512,1024]{1,0:T(8,128)(2,1)} fusion(bf16[2,4,1024,1024]{3,2,1,0:T(8,128)(2,1)} %param.6, f32[512]{0:T(512)S(1)} %bitcast.222, bf16[8,1024,512]{2,1,0:T(8,128)(2,1)} %all-gather.9.cloned.1.call-done), kind=kOutput, calls=%fused_computation.39 | convolution fusion | flops 2152726528 | bytes 6293504 | tf_op jit(solution)/shard_map/dot_general | solution.py:71
  259.7 3.2 fusion.109
  262.9 2.5 copy.42
  265.5 5.9 %convolution_convert_fusion.5 = bf16[512,1024]{1,0:T(8,128)(2,1)} fusion(bf16[2,4,1024,1024]{3,2,1,0:T(8,128)(2,1)} %param.6, f32[512]{0:T(512)S(1)} %bitcast.223, bf16[8,1024,512]{2,1,0:T(8,128)(2,1)} %all-gather.9.cloned.1.call-done), kind=kOutput, calls=%fused_computation.40 | convolution fusion | flops 2152726528 | bytes 6293504 | tf_op jit(solution)/shard_map/dot_general | solution.py:71
  271.4 3.2 fusion.107
  277.2 5.9 %convolution_convert_fusion.7 = bf16[512,1024]{1,0:T(8,128)(2,1)} fusion(bf16[2,4,1024,1024]{3,2,1,0:T(8,128)(2,1)} %param.6, f32[512]{0:T(512)S(1)} %bitcast.224, bf16[8,1024,512]{2,1,0:T(8,128)(2,1)} %all-gather.9.cloned.1.call-done), kind=kOutput, calls=%fused_computation.42 | convolution fusion | flops 2152726528 | bytes 6293504 | tf_op jit(solution)/shard_map/dot_general | solution.py:71
  283.1 3.2 fusion.103
  288.8 5.9 %convolution_convert_fusion.6 = bf16[512,1024]{1,0:T(8,128)(2,1)} fusion(bf16[2,4,1024,1024]{3,2,1,0:T(8,128)(2,1)} %param.6, f32[512]{0:T(512)S(1)} %bitcast.225, bf16[8,1024,512]{2,1,0:T(8,128)(2,1)} %all-gather.9.cloned.1.call-done), kind=kOutput, calls=%fused_computation.41 | convolution fusion | flops 2152726528 | bytes 6293504 | tf_op jit(solution)/shard_map/dot_general | solution.py:71
  294.7 3.3 fusion.105
  300.6 3.7 %fusion.33 = f32[512,512]{1,0:T(8,128)S(1)} fusion(f32[512,512]{1,0:T(8,128)} %fusion.108, f32[512,512]{0,1:T(8,128)} %copy.46, f32[512,512]{1,0:T(8,128)} %fusion.106, f32[512,512]{0,1:T(8,128)} %copy.45, f32[512,512]{1,0:T(8,128)S(1)} %fusion.104, f32[512,512]{0,1:T(8,128)} %copy.44, f32[512,512]{1,0:T(8,128)S(1)} %fusion.102, f32[512,512]{0,1:T(8,128)S(1)} %copy.43, ...), kind=kLoop, calls=%fused_computation.57 | loop fusion | flops 2883584 | bytes 9437200 | tf_op jit(solution)/shard_map/add | solution.py:78
  306.8 35.5 %all_to_all.5 = f32[32,2,16,512]{3,2,1,0:T(8,128)S(1)} all-to-all(f32[32,2,16,512]{3,2,1,0:T(8,128)S(1)} %maximum_bitcast_fusion), channel_id=1, replica_groups=mesh['tm'=4,'pair_0'=2,'pair_1'=4,'pair_2'=4] {'pair_0','pair_1','pair_2'}, dimensions={0} | all-to-all | bytes 4194304 | tf_op jit(solution)/shard_map/all_to_all | solution.py:39
  (50 shorter events, 22.8 us)
Async XLA Ops:
  6.5 43.8 %all-gather.5.cloned.1.call-start = ((), (), s32[]{:S(2)}) async-start(), calls=%async_computation.1 | async-start | bytes 2621440 | tf_op jit(solution)/shard_map/all_gather | solution.py:20
  17.5 117.6 %all-gather.7.cloned.1.call-start = ((), (), s32[]{:S(2)}) async-start(), calls=%async_computation.2 | async-start | bytes 10485760 | tf_op jit(solution)/shard_map/all_gather | solution.py:20
  50.4 163.0 %all-gather.9.cloned.1.call-start = ((), (), s32[]{:S(2)}) async-start(), calls=%async_computation.3 | async-start | bytes 10485760 | tf_op jit(solution)/shard_map/all_gather | solution.py:48
  147.0 1.7 copy-start.9
  147.0 1.7 copy-start.8
  300.5 3.8 %copy-start = (f32[512,512]{1,0:T(8,128)S(1)}, f32[512,512]{1,0:T(8,128)}, u32[]{:S(2)}) copy-start(f32[512,512]{1,0:T(8,128)} %fusion.109) | copy-start | bytes 3145732
  300.5 3.8 %copy-start.1 = (f32[512,512]{0,1:T(8,128)S(1)}, f32[512,512]{0,1:T(8,128)}, u32[]{:S(2)}) copy-start(f32[512,512]{0,1:T(8,128)} %copy.42) | copy-start | bytes 3145732
  300.5 3.8 %copy-start.2 = (f32[512,512]{1,0:T(8,128)S(1)}, f32[512,512]{1,0:T(8,128)}, u32[]{:S(2)}) copy-start(f32[512,512]{1,0:T(8,128)} %fusion.107) | copy-start | bytes 3145732
  300.5 3.8 %copy-start.3 = (f32[512,512]{0,1:T(8,128)S(1)}, f32[512,512]{0,1:T(8,128)}, u32[]{:S(2)}) copy-start(f32[512,512]{0,1:T(8,128)} %copy.41) | copy-start | bytes 3145732
  300.5 4.1 %copy-start.4 = (f32[512,512]{1,0:T(8,128)S(1)}, f32[512,512]{1,0:T(8,128)}, u32[]{:S(2)}) copy-start(f32[512,512]{1,0:T(8,128)} %fusion.103) | copy-start | bytes 3145732
  300.6 4.4 %copy-start.5 = (f32[512,512]{0,1:T(8,128)S(1)}, f32[512,512]{0,1:T(8,128)}, u32[]{:S(2)}) copy-start(f32[512,512]{0,1:T(8,128)} %copy.39) | copy-start | bytes 3145732
  300.6 4.7 %copy-start.6 = (f32[512,512]{1,0:T(8,128)S(1)}, f32[512,512]{1,0:T(8,128)}, u32[]{:S(2)}) copy-start(f32[512,512]{1,0:T(8,128)} %fusion.105) | copy-start | bytes 3145732
  300.6 4.9 %copy-start.7 = (f32[512,512]{0,1:T(8,128)S(1)}, f32[512,512]{0,1:T(8,128)}, u32[]{:S(2)}) copy-start(f32[512,512]{0,1:T(8,128)} %copy.40) | copy-start | bytes 3145732
Sparse Core Ops, SparseCore 0:
  17.6 32.7 all-gather.4
  52.0 83.0 all-gather.6
  148.8 64.5 all-gather.8
where the time goes:
time: 350 us
  waiting for transfers between devices  175 us (50%)
  matrix products  70 us (20%)
  blocking collectives  46.5 us (13%)
  local copies, waits for them, and re-layouts  31.8 us (9%)
  between operations  18.3 us (5%)
  other arithmetic  7.55 us (2%)
    all_gather x2, waiting for transfers between devices, stacked_from(): tiles = lax.all_gather(tiles, axes[k], axis=0, tiled=True)  117 us
    all_gather x1, waiting for transfers between devices, shards(): chosen = lax.all_gather(picked, 'tm', axis=2, tiled=True)  58.9 us
    dot_general x8, matrix products, shards(): lax.dot_general(left, product, (((0,), (0,)), ((), ())), preferred_elemen...  46.3 us
    all_to_all x1, blocking collectives, sum_at_owner(): tiles = lax.all_to_all(split_up(array, dim, count), axis, 0, 0, tiled=True)  35.5 us
    dot_general x8, matrix products, shards(): block = jnp.dot(half, right, preferred_element_type=jnp.float32)  23.6 us
    dot_general x8, local copies, waits for them, and re-layouts, shards(): block = jnp.dot(half, right, preferred_element_type=jnp.float32)  17.2 us
    all_gather x1, blocking collectives, stacked_from(): tiles = lax.all_gather(tiles, axes[k], axis=0, tiled=True)  10.9 us
    transpose x1, local copies, waits for them, and re-layouts, stacked_from(): tiles.transpose(*turned, *range(len(sequence), tiles.ndim))  7.53 us
  transfers between devices with their start and end apart: 3, of which 3 were waited for; matrix products, arithmetic and copies ran while one was open for 0% of the time, Pallas kernels for 0%

commit v1 on v0

--- a/solution.py
+++ b/solution.py
@@ -45,7 +45,10 @@
     wanted = pair_blocks.reshape(-1)
     narrow = whole_of(orbitals, PAIR, (0, 1, 2), 0)
     picked = jnp.take(narrow.reshape(-1, block_rows, narrow.shape[1]), wanted, axis=0)
-    chosen = lax.all_gather(picked, "tm", axis=2, tiled=True)
+    n_dev = lax.axis_size("tm")
+    blocks = jnp.stack([picked for _ in range(n_dev)])
+    blocks = lax.all_to_all(blocks, "tm", split_axis=0, concat_axis=0)
+    chosen = jnp.concatenate(blocks, axis=2)
     orbital_count = chosen.shape[2]
     time_local = screened.shape[0]
     pair_local = screened.shape[1]

time: 350 us -> 419 us (1.20)
  local copies, waits for them, and re-layouts: 31.8 us -> 64.2 us
  waiting for transfers between devices: 175 us -> 205 us
  starting transfers between devices: 0.08 us -> 6.05 us
    all_to_all x0 -> x1, waiting for transfers between devices: none -> 88.7 us  [shards(): blocks = lax.all_to_all(blocks, 'tm', split_axis=0, concat_axis=0)]
    all_gather x1 -> x0, waiting for transfers between devices: 58.9 us -> none  [shards(): chosen = lax.all_gather(picked, 'tm', axis=2, tiled=True)]
    slice x0 -> x9, local copies, waits for them, and re-layouts: none -> 20.1 us  [the longest x5 11 us: shards(): right = chosen[2 * pair_step + 1]]
    all_to_all x0 -> x1, local copies, waits for them, and re-layouts: none -> 7.53 us  [shards(): blocks = lax.all_to_all(blocks, 'tm', split_axis=0, concat_axis=0)]
    all_to_all x0 -> x1, starting transfers between devices: none -> 6 us  [shards(): blocks = lax.all_to_all(blocks, 'tm', split_axis=0, concat_axis=0)]
    another operation x0 -> x1, local copies, waits for them, and re-layouts: none -> 5.43 us  [shards(): blocks = jnp.stack([picked for _ in range(n_dev)])]
where the time goes in v1:
time: 419 us; the launch traced here: 418 us
  waiting for transfers between devices  205 us (49%)
  matrix products  71 us (17%)
  local copies, waits for them, and re-layouts  64.2 us (15%)
  blocking collectives  46.3 us (11%)
  between operations  18.6 us (4%)
  other arithmetic  6.78 us (2%)
  starting transfers between devices  6.05 us (1%)
    all_gather x2, waiting for transfers between devices, stacked_from(): tiles = lax.all_gather(tiles, axes[k], axis=0, tiled=True)  117 us
    all_to_all x1, waiting for transfers between devices, shards(): blocks = lax.all_to_all(blocks, 'tm', split_axis=0, concat_axis=0)  88.7 us
    dot_general x8, matrix products, shards(): lax.dot_general(left, product, (((0,), (0,)), ((), ())), preferred_elemen...  47.4 us
    all_to_all x1, blocking collectives, sum_at_owner(): tiles = lax.all_to_all(split_up(array, dim, count), axis, 0, 0, tiled=True)  35.4 us
    dot_general x8, matrix products, shards(): block = jnp.dot(half, right, preferred_element_type=jnp.float32)  23.6 us
    dot_general x8, local copies, waits for them, and re-layouts, shards(): block = jnp.dot(half, right, preferred_element_type=jnp.float32)  17.1 us
    slice x5, local copies, waits for them, and re-layouts, shards(): right = chosen[2 * pair_step + 1]  11 us
    all_gather x1, blocking collectives, stacked_from(): tiles = lax.all_gather(tiles, axes[k], axis=0, tiled=True)  10.9 us
  transfers between devices with their start and end apart: 3, of which 3 were waited for; matrix products, arithmetic and copies ran while one was open for 0% of the time, Pallas kernels for 0%

profile of v1, /device:TPU:0, one launch (start us, length us, event | category | flops | bytes accessed | tf_op | source)
XLA Modules:
  0.0 418.3 jit_solution(1424760639636686576)
XLA Ops:
  6.5 10.9 %all-gather = bf16[2048,128]{1,0:T(8,128)(2,1)} all-gather(bf16[1024,128]{1,0:T(8,128)(2,1)} %param.4), channel_id=2, replica_groups=mesh['tm'=4,'pair_0'=2,'pair_1'=4,'pair_2'=4] {'pair_0'}, dimensions={0}, use_global_device_ids=true | all-gather | bytes 786432 | tf_op jit(solution)/shard_map/all_gather | solution.py:20
  17.6 32.8 %all-gather.4.cloned.1.call-done = bf16[8,1024,128]{2,1,0:T(8,128)(2,1)} async-done(((bf16[2,1024,128]{2,1,0:T(8,128)(2,1)}), bf16[8,1024,128]{2,1,0:T(8,128)(2,1)}) %all-gather.4.cloned.1.call-update) | async-done | bytes 2097168 | tf_op jit(solution)/shard_map/all_gather | solution.py:20
  51.4 83.7 %all-gather.6.cloned.1.call-done = bf16[32,1024,128]{2,1,0:T(8,128)(2,1)} async-done(((bf16[8,1024,128]{2,1,0:T(8,128)(2,1)}), bf16[32,1024,128]{2,1,0:T(8,128)(2,1)}) %all-gather.6.cloned.1.call-update) | async-done | bytes 8388624 | tf_op jit(solution)/shard_map/all_gather | solution.py:20
  135.1 7.5 %copy.46 = bf16[2,4,4,1024,128]{4,3,2,1,0:T(8,128)(2,1)} copy(bf16[2,4,4,1024,128]{4,3,0,1,2:T(8,128)(2,1)} %bitcast.270) | data formatting | bytes 16777216 | tf_op jit(solution)/shard_map/transpose | solution.py:24
  142.6 4.3 %gather_fusion = bf16[8,1024,128]{2,1,0:T(8,128)(2,1)S(1)} fusion(bf16[32,1024,128]{2,1,0:T(8,128)(2,1)} %bitcast.269, s32[1024]{0:T(1024)S(1)} %pad_clamp_fusion), kind=kCustom, calls=%fused_computation | custom fusion | bytes 4194336 | tf_op jit(solution)/shard_map/jit(_take)/gather | solution.py:47
  147.2 5.4 %stack.16 = bf16[4,8,1024,128]{3,2,1,0:T(8,128)(2,1)} broadcast(bf16[8,1024,128]{2,1,0:T(8,128)(2,1)S(1)} %broadcast_select_fusion), dimensions={1,2,3} | broadcast | bytes 10485760 | tf_op jit(solution)/shard_map/stack | solution.py:49
  152.7 6.0 %all-to-all-start = ((bf16[4,8,1024,128]{3,2,1,0:T(8,128)(2,1)}), bf16[4,8,1024,128]{3,2,1,0:T(8,128)(2,1)}, u32[]{:S(2)}, u32[]{:S(2)}) async-start(bf16[4,8,1024,128]{3,2,1,0:T(8,128)(2,1)} %stack.16), calls=%async_computation | async-start | bytes 16777216 | tf_op jit(solution)/shard_map/all_to_all | solution.py:50
  164.5 88.7 %all-to-all-done = bf16[4,8,1024,128]{3,2,1,0:T(8,128)(2,1)} async-done(((bf16[4,8,1024,128]{3,2,1,0:T(8,128)(2,1)}), bf16[4,8,1024,128]{3,2,1,0:T(8,128)(2,1)}, u32[]{:S(2)}, u32[]{:S(2)}) %all-to-all-start) | async-done | bytes 8388640 | tf_op jit(solution)/shard_map/all_to_all | solution.py:50
  253.1 7.5 %copy.68 = bf16[4,8,1024,128]{3,2,0,1:T(8,128)(2,1)} copy(bf16[4,8,1024,128]{3,2,1,0:T(8,128)(2,1)} %all-to-all-done) | data formatting | bytes 16777216 | tf_op jit(solution)/shard_map/all_to_all | solution.py:50
  260.7 5.6 %fusion.136 = (bf16[1,1024,4,128]{3,1,2,0:T(8,128)(2,1)S(1)}, bf16[1,1024,4,128]{3,1,2,0:T(8,128)(2,1)S(1)}, bf16[1,1024,4,128]{3,1,2,0:T(8,128)(2,1)}, bf16[1,1...) fusion(bf16[8,1024,4,128]{3,1,2,0:T(8,128)(2,1)} %bitcast.260), kind=kLoop, calls=%fused_computation.115 | loop fusion | bytes 16777216 | tf_op jit(solution)/shard_map/slice | solution.py:66
  268.6 5.9 %convolution_convert_fusion = bf16[512,1024]{1,0:T(8,128)(2,1)} fusion(bf16[1024,512]{0,1:T(8,128)(2,1)} %bitcast.284, bf16[2,4,1024,1024]{3,2,1,0:T(8,128)(2,1)} %param.6, f32[4,128]{1,0:T(4,128)S(1)} %bitcast.294, bf16[8,1024,4,128]{3,1,2,0:T(8,128)(2,1)} %bitcast.261), kind=kOutput, calls=%fused_computation.36 | convolution fusion | flops 2152726528 | bytes 6293504 | tf_op jit(solution)/shard_map/dot_general | solution.py:74
  274.5 5.9 %convolution_convert_fusion.4 = bf16[512,1024]{1,0:T(8,128)(2,1)} fusion(bf16[1024,512]{0,1:T(8,128)(2,1)} %bitcast.285, bf16[2,4,1024,1024]{3,2,1,0:T(8,128)(2,1)} %param.6, f32[4,128]{1,0:T(4,128)S(1)} %bitcast.290, bf16[8,1024,4,128]{3,1,2,0:T(8,128)(2,1)} %bitcast.262), kind=kOutput, calls=%fused_computation.40 | convolution fusion | flops 2152726528 | bytes 6293504 | tf_op jit(solution)/shard_map/dot_general | solution.py:74
  282.7 5.9 %convolution_convert_fusion.1 = bf16[512,1024]{1,0:T(8,128)(2,1)} fusion(bf16[1024,512]{0,1:T(8,128)(2,1)} %bitcast.286, bf16[2,4,1024,1024]{3,2,1,0:T(8,128)(2,1)} %param.6, f32[4,128]{1,0:T(4,128)S(1)} %bitcast.295, bf16[8,1024,4,128]{3,1,2,0:T(8,128)(2,1)} %bitcast.263), kind=kOutput, calls=%fused_computation.37 | convolution fusion | flops 2152726528 | bytes 6293504 | tf_op jit(solution)/shard_map/dot_general | solution.py:74
  288.6 5.9 %convolution_convert_fusion.5 = bf16[512,1024]{1,0:T(8,128)(2,1)} fusion(bf16[1024,512]{0,1:T(8,128)(2,1)} %bitcast.287, bf16[2,4,1024,1024]{3,2,1,0:T(8,128)(2,1)} %param.6, f32[4,128]{1,0:T(4,128)S(1)} %bitcast.291, bf16[8,1024,4,128]{3,1,2,0:T(8,128)(2,1)} %bitcast.264), kind=kOutput, calls=%fused_computation.41 | convolution fusion | flops 2152726528 | bytes 6293504 | tf_op jit(solution)/shard_map/dot_general | solution.py:74
  296.8 5.9 %convolution_convert_fusion.2 = bf16[512,1024]{1,0:T(8,128)(2,1)} fusion(bf16[1024,512]{0,1:T(8,128)(2,1)} %bitcast.288, bf16[2,4,1024,1024]{3,2,1,0:T(8,128)(2,1)} %param.6, f32[4,128]{1,0:T(4,128)S(1)} %bitcast.296, bf16[8,1024,4,128]{3,1,2,0:T(8,128)(2,1)} %bitcast.265), kind=kOutput, calls=%fused_computation.38 | convolution fusion | flops 2152726528 | bytes 6293504 | tf_op jit(solution)/shard_map/dot_general | solution.py:74
  302.7 6.0 %convolution_convert_fusion.6 = bf16[512,1024]{1,0:T(8,128)(2,1)} fusion(bf16[1024,512]{0,1:T(8,128)(2,1)} %bitcast.289, bf16[2,4,1024,1024]{3,2,1,0:T(8,128)(2,1)} %param.6, f32[4,128]{1,0:T(4,128)S(1)} %bitcast.292, bf16[8,1024,4,128]{3,1,2,0:T(8,128)(2,1)} %bitcast.266), kind=kOutput, calls=%fused_computation.42 | convolution fusion | flops 2152726528 | bytes 6293504 | tf_op jit(solution)/shard_map/dot_general | solution.py:74
  310.9 6.0 %convolution_convert_fusion.3 = bf16[512,1024]{1,0:T(8,128)(2,1)} fusion(bf16[1024,512]{0,1:T(8,128)(2,1)} %bitcast.276, bf16[2,4,1024,1024]{3,2,1,0:T(8,128)(2,1)} %param.6, f32[4,128]{1,0:T(4,128)S(1)} %bitcast.297, bf16[8,1024,4,128]{3,1,2,0:T(8,128)(2,1)} %bitcast.267), kind=kOutput, calls=%fused_computation.39 | convolution fusion | flops 2152726528 | bytes 6293504 | tf_op jit(solution)/shard_map/dot_general | solution.py:74
  316.9 5.9 %convolution_convert_fusion.7 = bf16[512,1024]{1,0:T(8,128)(2,1)} fusion(bf16[1024,512]{0,1:T(8,128)(2,1)} %bitcast.277, bf16[2,4,1024,1024]{3,2,1,0:T(8,128)(2,1)} %param.6, f32[4,128]{1,0:T(4,128)S(1)} %bitcast.293, bf16[8,1024,4,128]{3,1,2,0:T(8,128)(2,1)} %bitcast.268), kind=kOutput, calls=%fused_computation.43 | convolution fusion | flops 2152726528 | bytes 6293504 | tf_op jit(solution)/shard_map/dot_general | solution.py:74
  334.7 3.3 fusion.145
  338.0 3.3 fusion.141
  357.2 3.3 fusion.139
  360.5 3.3 fusion.143
  369.0 4.3 %fusion.33 = f32[512,512]{1,0:T(8,128)S(1)} fusion(f32[512,512]{1,0:T(8,128)S(1)} %copy-done.2, f32[512,512]{0,1:T(8,128)} %copy.64, f32[512,512]{1,0:T(8,128)} %fusion.145, f32[512,512]{0,1:T(8,128)} %copy.63, f32[512,512]{1,0:T(8,128)} %fusion.144, f32[512,512]{0,1:T(8,128)} %copy.62, f32[512,512]{1,0:T(8,128)} %fusion.143, f32[512,512]{0,1:T(8,128)} %copy.61, ...), kind=kLoop, calls=%fused_computation.54 | loop fusion | flops 2883584 | bytes 9437200 | tf_op jit(solution)/shard_map/add | solution.py:81
  375.3 35.4 %all_to_all.10 = f32[32,2,16,512]{3,2,1,0:T(8,128)S(1)} all-to-all(f32[32,2,16,512]{3,2,1,0:T(8,128)S(1)} %maximum_bitcast_fusion), channel_id=1, replica_groups=mesh['tm'=4,'pair_0'=2,'pair_1'=4,'pair_2'=4] {'pair_0','pair_1','pair_2'}, dimensions={0} | all-to-all | bytes 4194304 | tf_op jit(solution)/shard_map/all_to_all | solution.py:39
  (60 shorter events, 46.8 us)
Async XLA Ops:
  6.5 43.8 %all-gather.4.cloned.1.call-start = ((), (), s32[]{:S(2)}) async-start(), calls=%async_computation.2 | async-start | bytes 2621440 | tf_op jit(solution)/shard_map/all_gather | solution.py:20
  17.5 117.6 %all-gather.6.cloned.1.call-start = ((), (), s32[]{:S(2)}) async-start(), calls=%async_computation.3 | async-start | bytes 10485760 | tf_op jit(solution)/shard_map/all_gather | solution.py:20
  152.7 6.0 %copy-start.9 = (f32[512]{0:T(512)S(1)}, f32[512]{0:T(512)}, u32[]{:S(2)}) copy-start(f32[512]{0:T(512)} %param.5) | copy-start | bytes 6148
  152.7 6.0 %copy-start.8 = (s32[4,2]{0,1:T(2,128)S(1)}, s32[4,2]{0,1:T(2,128)}, u32[]{:S(2)}) copy-start(s32[4,2]{0,1:T(2,128)} %param.7) | copy-start | bytes 100
  152.7 100.5 %all-to-all-start = ((bf16[4,8,1024,128]{3,2,1,0:T(8,128)(2,1)}), bf16[4,8,1024,128]{3,2,1,0:T(8,128)(2,1)}, u32[]{:S(2)}, u32[]{:S(2)}) async-start(bf16[4,8,1024,128]{3,2,1,0:T(8,128)(2,1)} %stack.16), calls=%async_computation | async-start | bytes 16777216 | tf_op jit(solution)/shard_map/all_to_all | solution.py:50
  353.3 3.9 copy-start.3
  360.5 8.5 %copy-start.2 = (f32[512,512]{1,0:T(8,128)S(1)}, f32[512,512]{1,0:T(8,128)}, u32[]{:S(2)}) copy-start(f32[512,512]{1,0:T(8,128)} %fusion.146) | copy-start | bytes 3145732
  369.0 4.4 %copy-start = (f32[512,512]{1,0:T(8,128)S(1)}, f32[512,512]{1,0:T(8,128)}, u32[]{:S(2)}) copy-start(f32[512,512]{1,0:T(8,128)} %fusion.141) | copy-start | bytes 3145732
  369.0 4.4 %copy-start.1 = (f32[512,512]{0,1:T(8,128)S(1)}, f32[512,512]{0,1:T(8,128)}, u32[]{:S(2)}) copy-start(f32[512,512]{0,1:T(8,128)} %copy.57) | copy-start | bytes 3145732
  369.0 4.4 %copy-start.4 = (f32[512,512]{1,0:T(8,128)S(1)}, f32[512,512]{1,0:T(8,128)}, u32[]{:S(2)}) copy-start(f32[512,512]{1,0:T(8,128)} %copy-done.3) | copy-start | bytes 3145732
  369.0 4.4 %copy-start.5 = (f32[512,512]{0,1:T(8,128)S(1)}, f32[512,512]{0,1:T(8,128)}, u32[]{:S(2)}) copy-start(f32[512,512]{0,1:T(8,128)} %copy.54) | copy-start | bytes 3145732
  369.0 4.6 %copy-start.6 = (f32[512,512]{1,0:T(8,128)S(1)}, f32[512,512]{1,0:T(8,128)}, u32[]{:S(2)}) copy-start(f32[512,512]{1,0:T(8,128)} %fusion.139) | copy-start | bytes 3145732
  369.0 4.9 %copy-start.7 = (f32[512,512]{0,1:T(8,128)S(1)}, f32[512,512]{0,1:T(8,128)}, u32[]{:S(2)}) copy-start(f32[512,512]{0,1:T(8,128)} %copy.51) | copy-start | bytes 3145732
Sparse Core Ops, SparseCore 0:
  17.6 32.7 all-gather.3
  52.0 83.0 all-gather.5
